TPU v7x, 256 devices: a whole 4x4x8 slice. The times are simulated.
256 devices in a mesh: gz: 4 (over x), grid: 64 (over y, z, core).
Axes of the slice: x: 4, y: 4, z: 8, core: 2. Of those that a mesh axis runs over, the one named last changes fastest.
Arguments:
- rhs: bfloat16 [6, 128, 32, 128], P(None, 'grid'), may hold values from -6 to 6
- lower_updates: bfloat16 [4, 6, 128, 32, 128], P('gz', None, 'grid'), may hold values from -6 to 6
- diag_inv: bfloat16 [6, 128, 128, 128], P(None, 'grid'), may hold values from -0.5 to 0.5
- lower_blocks: bfloat16 [5, 128, 128, 128], P(None, 'grid'), may hold values from -0.5 to 0.5
- upper_inv: bfloat16 [6, 128, 128, 128], P(None, 'grid'), may hold values from -0.5 to 0.5
- upper_blocks: bfloat16 [5, 128, 128, 128], P(None, 'grid'), may hold values from -0.5 to 0.5
- parent: int32 [5, 128], P(None, 'grid'), may hold values from 0 to 127, as said below
- live_count: int32 [6, 64], P(None, 'grid'), may hold values from 1 to 2
Outputs:
- solution: bfloat16 [6, 128, 32, 128], P(None, 'grid')
Inputs may be any that keep to these rules, and one draw needn't show every extreme that they name: At level l the slots form aligned groups of S = min(128, 4 * 2 * 2 ** l) slots (those of min(64, 4 * 2 ** l) grid indices in a row); parent[l, g] lies in the group of g, between (g // S) * S and (g // S) * S + S - 1, and both ends are named in every group.
All inputs are finite; a program needn't handle non-finite values.
Results may differ from a plain program's by a relative error of at most 0.03.
Values may be sent and summed in bfloat16 or wider, within the bound.
A program may use at most 64 MiB of HBM per device.

v0:
```python
import jax
import jax.numpy as jnp
from jax import lax
from jax.sharding import PartitionSpec as P


def on_device(
    rhs, lower_updates, diag_inv, lower_blocks, upper_inv, upper_blocks, parent, live_count
):
    f32 = jnp.float32
    bf16 = jnp.bfloat16
    levels, slots, rows, width = rhs.shape
    own_slots = lax.axis_index("grid") * slots + jnp.arange(slots, dtype=jnp.int32)
    live = (jnp.arange(slots, dtype=jnp.int32)[None, :] < live_count).astype(f32)
    updates = lax.psum(lower_updates[0].astype(f32).astype(jnp.bfloat16), "gz").astype(jnp.float32)
    flat = rows * width
    incoming = jnp.zeros((slots, rows, width), f32)
    forward_all = []
    for level in range(levels):
        residual = (rhs[level].astype(f32) - updates[level] - incoming).astype(bf16)
        forward = jnp.einsum("srw,swv->srv", residual, diag_inv[level], preferred_element_type=f32)
        forward = (forward * live[level][:, None, None]).astype(bf16)
        forward_all.append(forward)
        if level + 1 < levels:
            sent = jnp.einsum(
                "srw,swv->srv", forward, lower_blocks[level], preferred_element_type=f32
            )
            sent = sent.astype(bf16).reshape(slots, flat)
            targets = parent[level]
            values = lax.all_gather(sent, "grid", axis=0, tiled=True)
            owners = lax.all_gather(targets, "grid", axis=0, tiled=True)
            onehot = (owners[None, :] == own_slots[:, None]).astype(bf16)
            summed = jnp.dot(onehot, values, preferred_element_type=f32)
            incoming = summed.reshape(slots, rows, width)
    answer = [None] * levels
    upper_flat = None
    for level in range(levels - 1, -1, -1):
        if level == levels - 1:
            target = forward_all[level].astype(f32)
        else:
            targets = parent[level]

            def select_parent(total, piece, first, targets=targets):
                wanted = jnp.arange(piece.shape[0], dtype=jnp.int32)
                chosen = (targets[:, None] == wanted[None, :]).astype(bf16)
                return jnp.dot(chosen, piece, preferred_element_type=f32)

            above = select_parent(
                jnp.zeros((slots, flat), f32),
                lax.all_gather(upper_flat, "grid", axis=0, tiled=True),
                jnp.int32(0),
            )
            above = above.astype(bf16).reshape(slots, rows, width)
            target = forward_all[level].astype(f32) - jnp.einsum(
                "srw,swv->srv", above, upper_blocks[level], preferred_element_type=f32
            )
        target = target.astype(bf16)
        result = jnp.einsum("srw,swv->srv", target, upper_inv[level], preferred_element_type=f32)
        solved = (result * live[level][:, None, None]).astype(bf16)
        answer[level] = solved
        upper_flat = solved.reshape(slots, flat)
    stacked = jnp.stack(answer)
    return stacked


def solution(mesh):
    return jax.shard_map(
        on_device,
        mesh=mesh,
        in_specs=(
            P(None, "grid", None, None),
            P("gz", None, "grid", None, None),
            P(None, "grid", None, None),
            P(None, "grid", None, None),
            P(None, "grid", None, None),
            P(None, "grid", None, None),
            P(None, "grid"),
            P(None, "grid"),
        ),
        out_specs=P(None, "grid", None, None),
        check_vma=False,
    )
```

profile of v0, /device:TPU:1, one launch (start us, length us, event | category | flops | bytes accessed | tf_op | source)
XLA Modules:
  0.0 849.4 jit_solution(444018859633957401)
XLA Ops:
  6.5 0.7 all-reduce.8.cloned.1.call-update
  7.3 0.7 fusion.132
  8.0 49.8 %all-reduce.8.cloned.1.call-done = bf16[6,2,32,128]{3,2,1,0:T(8,128)(2,1)} async-done(((bf16[6,2,32,128]{3,2,1,0:T(8,128)(2,1)}), bf16[6,2,32,128]{3,2,1,0:T(8,128)(2,1)}) %all-reduce.8.cloned.1.call-update) | async-done | bytes 98320 | tf_op jit(solution)/shard_map/psum | solution.py:15
  57.8 0.9 convert_element_type.162
  58.7 0.8 fusion
  59.5 1.0 convolution_convert_fusion.9
  60.5 0.6 reshape.133
  61.3 0.7 copy-done.7
  61.9 0.6 dynamic-slice
  63.2 0.2 slice_reduce_fusion
  63.5 0.2 dynamic-update-slice.4
  63.7 0.2 dynamic-update-slice.2
  63.9 0.2 dynamic-update-slice.1
  64.5 19.4 %all-reduce.5 = (s32[128]{0:T(128)S(1)}, s32[128]{0:T(128)S(1)}, s32[128]{0:T(128)S(1)}, s32[128]{0:T(128)S(1)}, s32[128]{0:T(128)S(1)}) all-reduce(s32[128]{0:T(128)S(1)} %dynamic-update-slice, s32[128]{0:T(128)S(1)} %dynamic-update-slice.1, s32[128]{0:T(128)S(1)} %dynamic-update-slice.2, ...), channel_id=2, replica_groups=mesh['gz'=4,'grid'=64] {'grid'}, use_global_device_ids=true, to_apply=%add | all-reduce | flops 640 | bytes 5120
  83.9 57.2 %all-gather.26.cloned.1.call-done = bf16[64,2,4096]{2,1,0:T(2,128)(2,1)} async-done(((bf16[1,2,4096]{2,1,0:T(2,128)(2,1)}), bf16[64,2,4096]{2,1,0:T(2,128)(2,1)}) %all-gather.26.cloned.1.call-update) | async-done | bytes 1048592 | tf_op jit(solution)/shard_map/all_gather | solution.py:30
  141.1 1.5 reshape.134
  142.6 0.3 convolution_bitcast_fusion.4
  142.9 0.6 copy-done.2
  143.7 0.6 reshape.135
  144.4 74.7 %all-gather.28.cloned.1.call-done = bf16[64,2,4096]{2,1,0:T(2,128)(2,1)} async-done(((bf16[1,2,4096]{2,1,0:T(2,128)(2,1)}), bf16[64,2,4096]{2,1,0:T(2,128)(2,1)}) %all-gather.28.cloned.1.call-update) | async-done | bytes 1048592 | tf_op jit(solution)/shard_map/all_gather | solution.py:30
  219.1 1.5 reshape.136
  220.5 0.3 convolution_bitcast_fusion.3
  221.1 0.6 reshape.137
  221.8 74.7 %all-gather.30.cloned.1.call-done = bf16[64,2,4096]{2,1,0:T(2,128)(2,1)} async-done(((bf16[1,2,4096]{2,1,0:T(2,128)(2,1)}), bf16[64,2,4096]{2,1,0:T(2,128)(2,1)}) %all-gather.30.cloned.1.call-update) | async-done | bytes 1048592 | tf_op jit(solution)/shard_map/all_gather | solution.py:30
  296.5 1.5 reshape.138
  297.9 0.3 convolution_bitcast_fusion.2
  298.5 0.6 reshape.139
  299.2 74.7 %all-gather.32.cloned.1.call-done = bf16[64,2,4096]{2,1,0:T(2,128)(2,1)} async-done(((bf16[1,2,4096]{2,1,0:T(2,128)(2,1)}), bf16[64,2,4096]{2,1,0:T(2,128)(2,1)}) %all-gather.32.cloned.1.call-update) | async-done | bytes 1048592 | tf_op jit(solution)/shard_map/all_gather | solution.py:30
  373.9 1.5 reshape.140
  375.4 0.3 convolution_bitcast_fusion.1
  375.9 0.6 reshape.141
  376.6 74.7 %all-gather.34.cloned.1.call-done = bf16[64,2,4096]{2,1,0:T(2,128)(2,1)} async-done(((bf16[1,2,4096]{2,1,0:T(2,128)(2,1)}), bf16[64,2,4096]{2,1,0:T(2,128)(2,1)}) %all-gather.34.cloned.1.call-update) | async-done | bytes 1048592 | tf_op jit(solution)/shard_map/all_gather | solution.py:30
  451.3 1.5 reshape.142
  452.8 0.3 convolution_bitcast_fusion
  453.1 0.7 copy-done.4
  453.8 0.2 fusion.6
  454.0 0.7 reshape.143
  454.7 74.7 %all-gather.36.cloned.1.call-done = bf16[64,2,4096]{2,1,0:T(2,128)(2,1)} async-done(((bf16[1,2,4096]{2,1,0:T(2,128)(2,1)}), bf16[64,2,4096]{2,1,0:T(2,128)(2,1)}) %all-gather.36.cloned.1.call-update) | async-done | bytes 1048592 | tf_op jit(solution)/shard_map/all_gather | solution.py:50
  529.4 1.5 reshape.144
  530.8 0.3 fusion.19
  531.1 0.7 copy-done.5
  531.8 0.2 fusion.8
  532.0 0.7 reshape.145
  532.8 74.7 %all-gather.38.cloned.1.call-done = bf16[64,2,4096]{2,1,0:T(2,128)(2,1)} async-done(((bf16[1,2,4096]{2,1,0:T(2,128)(2,1)}), bf16[64,2,4096]{2,1,0:T(2,128)(2,1)}) %all-gather.38.cloned.1.call-update) | async-done | bytes 1048592 | tf_op jit(solution)/shard_map/all_gather | solution.py:50
  607.4 1.5 reshape.146
  608.9 0.3 fusion.20
  609.2 0.2 fusion.10
  609.4 0.7 reshape.147
  610.1 74.7 %all-gather.40.cloned.1.call-done = bf16[64,2,4096]{2,1,0:T(2,128)(2,1)} async-done(((bf16[1,2,4096]{2,1,0:T(2,128)(2,1)}), bf16[64,2,4096]{2,1,0:T(2,128)(2,1)}) %all-gather.40.cloned.1.call-update) | async-done | bytes 1048592 | tf_op jit(solution)/shard_map/all_gather | solution.py:50
  684.8 1.5 reshape.148
  686.3 0.3 fusion.21
  686.6 0.2 fusion.12
  686.8 0.7 reshape.149
  687.5 74.7 %all-gather.42.cloned.1.call-done = bf16[64,2,4096]{2,1,0:T(2,128)(2,1)} async-done(((bf16[1,2,4096]{2,1,0:T(2,128)(2,1)}), bf16[64,2,4096]{2,1,0:T(2,128)(2,1)}) %all-gather.42.cloned.1.call-update) | async-done | bytes 1048592 | tf_op jit(solution)/shard_map/all_gather | solution.py:50
  762.2 1.5 reshape.150
  763.7 0.3 fusion.22
  764.0 0.2 fusion.14
  764.2 0.7 reshape.151
  764.9 74.7 %all-gather.44.cloned.1.call-done = bf16[64,2,4096]{2,1,0:T(2,128)(2,1)} async-done(((bf16[1,2,4096]{2,1,0:T(2,128)(2,1)}), bf16[64,2,4096]{2,1,0:T(2,128)(2,1)}) %all-gather.44.cloned.1.call-update) | async-done | bytes 1048592 | tf_op jit(solution)/shard_map/all_gather | solution.py:50
  839.6 1.5 reshape.152
  841.0 0.3 fusion.23
  841.4 0.2 fusion.18
  841.7 0.6 copy-done.6
  842.3 0.6 bitcast_dynamic-update-slice_fusion
  (53 shorter events, 2.2 us)
Async XLA Ops:
  6.5 52.2 %copy-start = (bf16[6,2,128,128]{3,2,1,0:T(8,128)(2,1)S(1)}, bf16[6,2,128,128]{3,2,1,0:T(8,128)(2,1)}, u32[]{:S(2)}) copy-start(bf16[6,2,128,128]{3,2,1,0:T(8,128)(2,1)} %param.10) | copy-start | bytes 1179652
  6.5 51.3 %all-reduce.8.cloned.1.call-start = ((), (), s32[]{:S(2)}) async-start(), calls=%async_computation | async-start | bytes 196608 | tf_op jit(solution)/shard_map/psum | solution.py:15
  7.3 133.8 %all-gather.26.cloned.1.call-start = ((), (), s32[]{:S(2)}) async-start(), calls=%async_computation.1 | async-start | bytes 1064960 | tf_op jit(solution)/shard_map/all_gather | solution.py:30
  61.2 157.9 %all-gather.28.cloned.1.call-start = ((), (), s32[]{:S(2)}) async-start(), calls=%async_computation.2 | async-start | bytes 1064960 | tf_op jit(solution)/shard_map/all_gather | solution.py:30
  61.2 0.7 copy-start.7
  62.5 0.7 copy-start.3
  142.5 0.9 copy-start.2
  142.6 1.0 copy-start.1
  144.4 152.1 %all-gather.30.cloned.1.call-start = ((), (), s32[]{:S(2)}) async-start(), calls=%async_computation.3 | async-start | bytes 1064960 | tf_op jit(solution)/shard_map/all_gather | solution.py:30
  221.8 152.1 %all-gather.32.cloned.1.call-start = ((), (), s32[]{:S(2)}) async-start(), calls=%async_computation.4 | async-start | bytes 1064960 | tf_op jit(solution)/shard_map/all_gather | solution.py:30
  299.2 152.1 %all-gather.34.cloned.1.call-start = ((), (), s32[]{:S(2)}) async-start(), calls=%async_computation.5 | async-start | bytes 1064960 | tf_op jit(solution)/shard_map/all_gather | solution.py:30
  376.6 152.8 %all-gather.36.cloned.1.call-start = ((), (), s32[]{:S(2)}) async-start(), calls=%async_computation.6 | async-start | bytes 1064960 | tf_op jit(solution)/shard_map/all_gather | solution.py:50
  452.8 1.0 copy-start.4
  454.7 152.8 %all-gather.38.cloned.1.call-start = ((), (), s32[]{:S(2)}) async-start(), calls=%async_computation.7 | async-start | bytes 1064960 | tf_op jit(solution)/shard_map/all_gather | solution.py:50
  530.8 1.0 copy-start.5
  532.7 152.1 %all-gather.40.cloned.1.call-start = ((), (), s32[]{:S(2)}) async-start(), calls=%async_computation.8 | async-start | bytes 1064960 | tf_op jit(solution)/shard_map/all_gather | solution.py:50
  610.1 152.1 %all-gather.42.cloned.1.call-start = ((), (), s32[]{:S(2)}) async-start(), calls=%async_computation.9 | async-start | bytes 1064960 | tf_op jit(solution)/shard_map/all_gather | solution.py:50
  687.5 152.1 %all-gather.44.cloned.1.call-start = ((), (), s32[]{:S(2)}) async-start(), calls=%async_computation.10 | async-start | bytes 1064960 | tf_op jit(solution)/shard_map/all_gather | solution.py:50
  841.7 0.6 copy-start.6
Sparse Core Ops, SparseCore 0:
  9.6 48.1 all-reduce.7
  61.3 79.7 all-gather.25
  144.5 74.5 all-gather.27
  221.9 74.5 all-gather.29
  299.3 74.5 all-gather.31
  376.7 74.5 all-gather.33
  454.8 74.5 all-gather.35
  532.8 74.5 all-gather.37
  610.2 74.5 all-gather.39
  687.6 74.5 all-gather.41
  765.0 74.5 all-gather.43
where the time goes:
time: 850 us; the launch traced here: 849 us
  waiting for transfers between devices  780 us (92%)
  local copies, waits for them, and re-layouts  27 us (3%)
  blocking collectives  19.4 us (2%)
  between operations  14.1 us (2%)
    all_gather x5, waiting for transfers between devices, on_device(): lax.all_gather(upper_flat, 'grid', axis=0, tiled=True)  373 us
    all_gather x5, waiting for transfers between devices, on_device(): values = lax.all_gather(sent, 'grid', axis=0, tiled=True)  356 us
    psum x1, waiting for transfers between devices, on_device(): lax.psum(lower_updates[0].astype(f32).astype(jnp.bfloat16), 'gz')  49.8 us
    unnamed x51, local copies, waits for them, and re-layouts  26.1 us
    unnamed x1, blocking collectives  19.4 us
  transfers between devices with their start and end apart: 11, of which 11 were waited for; matrix products, arithmetic and copies ran while one was open for 0% of the time, Pallas kernels for 0%

commit v1 on v0

--- a/solution.py
+++ b/solution.py
@@ -12,7 +12,10 @@
     levels, slots, rows, width = rhs.shape
     own_slots = lax.axis_index("grid") * slots + jnp.arange(slots, dtype=jnp.int32)
     live = (jnp.arange(slots, dtype=jnp.int32)[None, :] < live_count).astype(f32)
-    updates = lax.psum(lower_updates[0].astype(f32).astype(jnp.bfloat16), "gz").astype(jnp.float32)
+    edge_follow = lambda message, mesh_ax: lax.all_gather(message, axis_name=mesh_ax).sum(axis=0)
+    updates = edge_follow(lower_updates[0].astype(f32).astype(jnp.bfloat16), mesh_ax="gz").astype(
+        jnp.float32
+    )
     flat = rows * width
     incoming = jnp.zeros((slots, rows, width), f32)
     forward_all = []

time: 850 us -> 812 us (0.955)
  waiting for transfers between devices: 780 us -> 729 us
  blocking collectives: 19.4 us -> 34 us
    psum x1 -> x0, waiting for transfers between devices: 49.8 us -> none  [on_device(): lax.psum(lower_updates[0].astype(f32).astype(jnp.bfloat16), 'gz')]
    all_gather x0 -> x1, blocking collectives: none -> 11.9 us  [on_device(): lax.all_gather(message, axis_name=mesh_ax).sum(axis=0)]
    unnamed x51 -> x53, local copies, waits for them, and re-layouts: 26.1 us -> 27.2 us
  transfers between devices with their start and end apart: 11 -> 10, of which waited for: 11 -> 10; matrix products, arithmetic and copies ran while one was open for 0% -> 0% of each run, Pallas kernels for 0% -> 0%
where the time goes in v1:
time: 812 us; the launch traced here: 811 us
  waiting for transfers between devices  729 us (90%)
  blocking collectives  34 us (4%)
  local copies, waits for them, and re-layouts  28 us (3%)
  between operations  14.3 us (2%)
    all_gather x5, waiting for transfers between devices, on_device(): lax.all_gather(upper_flat, 'grid', axis=0, tiled=True)  373 us
    all_gather x5, waiting for transfers between devices, on_device(): values = lax.all_gather(sent, 'grid', axis=0, tiled=True)  355 us
    unnamed x53, local copies, waits for them, and re-layouts  27.2 us
    unnamed x1, blocking collectives  22.1 us
  transfers between devices with their start and end apart: 10, of which 10 were waited for; matrix products, arithmetic and copies ran while one was open for 0% of the time, Pallas kernels for 0%

profile of v1, /device:TPU:1, one launch (start us, length us, event | category | flops | bytes accessed | tf_op | source)
XLA Modules:
  0.0 811.3 jit_solution(809467203784156283)
XLA Ops:
  6.5 0.7 copy-done.5
  7.3 11.9 %all_gather.49 = bf16[4,6,2,32,128]{4,3,2,1,0:T(8,128)(2,1)S(1)} all-gather(bf16[1,6,2,32,128]{4,3,2,1,0:T(8,128)(2,1)} %param.9), channel_id=1, replica_groups=mesh['gz'=4,'grid'=64] {'gz'}, dimensions={0}, use_global_device_ids=true | all-gather | bytes 491520 | tf_op jit(solution)/shard_map/all_gather | solution.py:15
  19.3 0.9 copy-done
  20.5 0.6 reshape.134
  21.2 0.7 copy-done.8
  21.8 0.6 dynamic-slice
  23.1 0.2 slice_reduce_fusion
  23.3 0.2 dynamic-update-slice.4
  23.6 0.2 dynamic-update-slice.2
  23.8 0.2 dynamic-update-slice.1
  24.0 0.2 dynamic-update-slice
  24.2 0.2 dynamic-update-slice.3
  24.4 22.1 %all-reduce.5 = (s32[128]{0:T(128)S(1)}, s32[128]{0:T(128)S(1)}, s32[128]{0:T(128)S(1)}, s32[128]{0:T(128)S(1)}, s32[128]{0:T(128)S(1)}) all-reduce(s32[128]{0:T(128)S(1)} %dynamic-update-slice, s32[128]{0:T(128)S(1)} %dynamic-update-slice.1, s32[128]{0:T(128)S(1)} %dynamic-update-slice.2, ...), channel_id=2, replica_groups=mesh['gz'=4,'grid'=64] {'grid'}, use_global_device_ids=true, to_apply=%add | all-reduce | flops 640 | bytes 5120
  46.5 56.7 %all-gather.26.cloned.1.call-done = bf16[64,2,4096]{2,1,0:T(2,128)(2,1)} async-done(((bf16[1,2,4096]{2,1,0:T(2,128)(2,1)}), bf16[64,2,4096]{2,1,0:T(2,128)(2,1)}) %all-gather.26.cloned.1.call-update) | async-done | bytes 1048592 | tf_op jit(solution)/shard_map/all_gather | solution.py:33
  103.2 1.5 reshape.135
  104.7 0.3 convolution_bitcast_fusion.4
  105.1 0.2 convolution_convert_fusion.8
  105.3 0.6 reshape.136
  106.0 74.7 %all-gather.28.cloned.1.call-done = bf16[64,2,4096]{2,1,0:T(2,128)(2,1)} async-done(((bf16[1,2,4096]{2,1,0:T(2,128)(2,1)}), bf16[64,2,4096]{2,1,0:T(2,128)(2,1)}) %all-gather.28.cloned.1.call-update) | async-done | bytes 1048592 | tf_op jit(solution)/shard_map/all_gather | solution.py:33
  180.6 1.5 reshape.137
  182.1 0.3 convolution_bitcast_fusion.3
  182.5 0.2 convolution_convert_fusion.7
  182.7 0.6 reshape.138
  183.4 74.7 %all-gather.30.cloned.1.call-done = bf16[64,2,4096]{2,1,0:T(2,128)(2,1)} async-done(((bf16[1,2,4096]{2,1,0:T(2,128)(2,1)}), bf16[64,2,4096]{2,1,0:T(2,128)(2,1)}) %all-gather.30.cloned.1.call-update) | async-done | bytes 1048592 | tf_op jit(solution)/shard_map/all_gather | solution.py:33
  258.0 1.5 reshape.139
  259.5 0.3 convolution_bitcast_fusion.2
  260.1 0.6 reshape.140
  260.8 74.7 %all-gather.32.cloned.1.call-done = bf16[64,2,4096]{2,1,0:T(2,128)(2,1)} async-done(((bf16[1,2,4096]{2,1,0:T(2,128)(2,1)}), bf16[64,2,4096]{2,1,0:T(2,128)(2,1)}) %all-gather.32.cloned.1.call-update) | async-done | bytes 1048592 | tf_op jit(solution)/shard_map/all_gather | solution.py:33
  335.4 1.5 reshape.141
  336.9 0.3 convolution_bitcast_fusion.1
  337.5 0.6 reshape.142
  338.2 74.7 %all-gather.34.cloned.1.call-done = bf16[64,2,4096]{2,1,0:T(2,128)(2,1)} async-done(((bf16[1,2,4096]{2,1,0:T(2,128)(2,1)}), bf16[64,2,4096]{2,1,0:T(2,128)(2,1)}) %all-gather.34.cloned.1.call-update) | async-done | bytes 1048592 | tf_op jit(solution)/shard_map/all_gather | solution.py:33
  412.8 1.5 reshape.143
  414.3 0.3 convolution_bitcast_fusion
  414.6 0.7 copy-done.4
  415.3 0.2 fusion.6
  415.5 0.7 reshape.144
  416.3 74.7 %all-gather.36.cloned.1.call-done = bf16[64,2,4096]{2,1,0:T(2,128)(2,1)} async-done(((bf16[1,2,4096]{2,1,0:T(2,128)(2,1)}), bf16[64,2,4096]{2,1,0:T(2,128)(2,1)}) %all-gather.36.cloned.1.call-update) | async-done | bytes 1048592 | tf_op jit(solution)/shard_map/all_gather | solution.py:53
  490.9 1.5 reshape.145
  492.4 0.3 fusion.19
  492.7 0.7 copy-done.6
  493.4 0.2 fusion.8
  493.6 0.7 reshape.146
  494.3 74.7 %all-gather.38.cloned.1.call-done = bf16[64,2,4096]{2,1,0:T(2,128)(2,1)} async-done(((bf16[1,2,4096]{2,1,0:T(2,128)(2,1)}), bf16[64,2,4096]{2,1,0:T(2,128)(2,1)}) %all-gather.38.cloned.1.call-update) | async-done | bytes 1048592 | tf_op jit(solution)/shard_map/all_gather | solution.py:53
  569.0 1.5 reshape.147
  570.4 0.3 fusion.20
  570.7 0.2 fusion.10
  571.0 0.7 reshape.148
  571.7 74.7 %all-gather.40.cloned.1.call-done = bf16[64,2,4096]{2,1,0:T(2,128)(2,1)} async-done(((bf16[1,2,4096]{2,1,0:T(2,128)(2,1)}), bf16[64,2,4096]{2,1,0:T(2,128)(2,1)}) %all-gather.40.cloned.1.call-update) | async-done | bytes 1048592 | tf_op jit(solution)/shard_map/all_gather | solution.py:53
  646.4 1.5 reshape.149
  647.8 0.3 fusion.21
  648.1 0.2 fusion.12
  648.3 0.7 reshape.150
  649.1 74.7 %all-gather.42.cloned.1.call-done = bf16[64,2,4096]{2,1,0:T(2,128)(2,1)} async-done(((bf16[1,2,4096]{2,1,0:T(2,128)(2,1)}), bf16[64,2,4096]{2,1,0:T(2,128)(2,1)}) %all-gather.42.cloned.1.call-update) | async-done | bytes 1048592 | tf_op jit(solution)/shard_map/all_gather | solution.py:53
  723.7 1.5 reshape.151
  725.2 0.3 fusion.22
  725.5 0.2 fusion.14
  725.7 0.7 reshape.152
  726.4 74.7 %all-gather.44.cloned.1.call-done = bf16[64,2,4096]{2,1,0:T(2,128)(2,1)} async-done(((bf16[1,2,4096]{2,1,0:T(2,128)(2,1)}), bf16[64,2,4096]{2,1,0:T(2,128)(2,1)}) %all-gather.44.cloned.1.call-update) | async-done | bytes 1048592 | tf_op jit(solution)/shard_map/all_gather | solution.py:53
  801.1 1.5 reshape.153
  802.6 0.3 fusion.23
  802.9 0.2 fusion.18
  803.2 0.6 copy-done.7
  803.8 0.6 bitcast_dynamic-update-slice_fusion
  (54 shorter events, 1.9 us)
Async XLA Ops:
  6.5 0.7 copy-start.5
  6.5 96.7 %all-gather.26.cloned.1.call-start = ((), (), s32[]{:S(2)}) async-start(), calls=%async_computation | async-start | bytes 1064960 | tf_op jit(solution)/shard_map/all_gather | solution.py:33
  19.2 1.0 copy-start
  19.2 1.0 copy-start.2
  19.2 1.1 copy-start.1
  21.1 159.5 %all-gather.28.cloned.1.call-start = ((), (), s32[]{:S(2)}) async-start(), calls=%async_computation.1 | async-start | bytes 1064960 | tf_op jit(solution)/shard_map/all_gather | solution.py:33
  21.2 0.7 copy-start.8
  22.4 0.7 copy-start.3
  105.9 152.1 %all-gather.30.cloned.1.call-start = ((), (), s32[]{:S(2)}) async-start(), calls=%async_computation.2 | async-start | bytes 1064960 | tf_op jit(solution)/shard_map/all_gather | solution.py:33
  183.3 152.1 %all-gather.32.cloned.1.call-start = ((), (), s32[]{:S(2)}) async-start(), calls=%async_computation.3 | async-start | bytes 1064960 | tf_op jit(solution)/shard_map/all_gather | solution.py:33
  260.7 152.1 %all-gather.34.cloned.1.call-start = ((), (), s32[]{:S(2)}) async-start(), calls=%async_computation.4 | async-start | bytes 1064960 | tf_op jit(solution)/shard_map/all_gather | solution.py:33
  338.1 152.8 %all-gather.36.cloned.1.call-start = ((), (), s32[]{:S(2)}) async-start(), calls=%async_computation.5 | async-start | bytes 1064960 | tf_op jit(solution)/shard_map/all_gather | solution.py:53
  414.3 1.0 copy-start.4
  416.2 152.8 %all-gather.38.cloned.1.call-start = ((), (), s32[]{:S(2)}) async-start(), calls=%async_computation.6 | async-start | bytes 1064960 | tf_op jit(solution)/shard_map/all_gather | solution.py:53
  492.4 1.0 copy-start.6
  494.3 152.1 %all-gather.40.cloned.1.call-start = ((), (), s32[]{:S(2)}) async-start(), calls=%async_computation.7 | async-start | bytes 1064960 | tf_op jit(solution)/shard_map/all_gather | solution.py:53
  571.6 152.1 %all-gather.42.cloned.1.call-start = ((), (), s32[]{:S(2)}) async-start(), calls=%async_computation.8 | async-start | bytes 1064960 | tf_op jit(solution)/shard_map/all_gather | solution.py:53
  649.0 152.1 %all-gather.44.cloned.1.call-start = ((), (), s32[]{:S(2)}) async-start(), calls=%async_computation.9 | async-start | bytes 1064960 | tf_op jit(solution)/shard_map/all_gather | solution.py:53
  803.2 0.6 copy-start.7
Sparse Core Ops, SparseCore 0:
  21.2 81.9 all-gather.25
  106.0 74.5 all-gather.27
  183.4 74.5 all-gather.29
  260.8 74.5 all-gather.31
  338.2 74.5 all-gather.33
  416.3 74.5 all-gather.35
  494.4 74.5 all-gather.37
  571.8 74.5 all-gather.39
  649.2 74.5 all-gather.41
  726.5 74.5 all-gather.43
